TPU v7x, 256 devices: a whole 4x4x8 slice. The times are simulated.
256 devices in a mesh: row: 64 (over y, z, core), col: 4 (over x).
Axes of the slice: x: 4, y: 4, z: 8, core: 2. Of those that a mesh axis runs over, the one named last changes fastest.
Arguments:
- factor: float32 [8192, 8192], P('row', 'col'), may hold values from -0.125 to 0.125
- rhs: float32 [8192, 512], P('row', 'col'), may hold values from -6 to 6
- parent: int32 [7], replicated, may hold values from 4 to 6, as said below
- bounds: int32 [8], replicated, may hold values from 0 to 64, as said below
- slot: int32 [64], replicated, may hold values from 0 to 63, each once
- structure: int32 [7, 64], replicated, may hold values 0 or 1
Outputs:
- solution: float32 [8192, 512], P('row', 'col')
Inputs may be any that keep to these rules, and one draw needn't show every extreme that they name: parent[s] is 4 or 5 for s = 0 to 3, and 6 for s = 4, 5, 6 (the root is its own entry). bounds[0] = 0, bounds[7] = 64, strictly increasing; supernode s holds logical blocks bounds[s] to bounds[s+1] - 1. `slot`: a permutation.
All inputs are finite; a program needn't handle non-finite values.
Results may differ from a plain program's by a relative error of at most 0.0001.
Values sent between devices are 32-bit elements; how exact they have to be, the bound alone decides.
A program may use at most 64 MiB of HBM per device.

v0:
```python
import jax
import jax.numpy as jnp
from jax import lax
from jax.sharding import PartitionSpec as P

B = 128
RB = 1


def block_masks(parent, bounds, slot, structure):
    count = slot.shape[0]
    ar = jnp.arange(count, dtype=jnp.int32)
    logical = jnp.sum(jnp.where(slot[:, None] == ar[None, :], ar[:, None], 0), axis=0)
    node = jnp.sum((logical[:, None] >= bounds[None, 1:7]).astype(jnp.int32), axis=1)
    level = (node >= 4).astype(jnp.int32) + (node >= 6).astype(jnp.int32)
    nodes = jnp.arange(7, dtype=jnp.int32)
    grand = parent[parent]
    ancestor = ((nodes[None, :] == parent[:, None]) | (nodes[None, :] == grand[:, None])) & (
        nodes[None, :] != nodes[:, None]
    )
    node_hot = (node[:, None] == nodes[None, :]).astype(jnp.float32)
    perm_hot = (logical[:, None] == ar[None, :]).astype(jnp.float32)
    listed_store = jnp.dot(
        structure.astype(jnp.float32), perm_hot.T, precision=lax.Precision.HIGHEST
    )
    anc_pairs = jnp.dot(
        node_hot,
        jnp.dot(ancestor.astype(jnp.float32), node_hot.T, precision=lax.Precision.HIGHEST),
        precision=lax.Precision.HIGHEST,
    )
    list_pairs = jnp.dot(node_hot, listed_store, precision=lax.Precision.HIGHEST)
    link = (anc_pairs * list_pairs).T > 0.5
    same = node[:, None] == node[None, :]
    return (level, same, link)


def masked(block_rows, mask):
    rblocks, width = mask.shape
    bsz = block_rows.shape[0] // rblocks
    shaped = block_rows.reshape(rblocks, bsz, width, bsz) * mask[:, None, :, None].astype(
        jnp.float32
    )
    return shaped.reshape(block_rows.shape)


def body(factor, rhs, parent, bounds, slot, structure):
    level, same, link = block_masks(parent, bounds, slot, structure)
    first = lax.axis_index("row") * RB
    level_mine = lax.dynamic_slice_in_dim(level, first, RB, 0)
    same_mine = lax.dynamic_slice_in_dim(same, first, RB, 0)
    link_mine = lax.dynamic_slice_in_dim(link, first, RB, 0)
    full_rows = lax.all_gather(factor, "col", axis=1, tiled=True)
    diag_part = masked(full_rows, same_mine)
    link_part = masked(full_rows, link_mine)

    def product(matrix, vector):
        return jnp.dot(
            matrix,
            lax.all_gather(vector, "row", axis=0, tiled=True),
            precision=lax.Precision.HIGHEST,
            preferred_element_type=jnp.float32,
        )

    pieces = [rhs]
    accums = [jnp.zeros(p.shape, jnp.float32) for p in pieces]
    results = [jnp.zeros(p.shape, jnp.float32) for p in pieces]
    for section in range(3):
        rows = jnp.repeat(level_mine == section, B)[:, None]
        solved = jnp.where(rows, product(diag_part, pieces[0] - accums[0]), 0.0)
        results[0] = results[0] + solved
        if section < 2:
            accums[0] = accums[0] + product(link_part, solved)
    return results[0]


def solution(mesh):
    in_specs = (P("row", "col"), P("row", "col"), P(), P(), P(), P())
    out_specs = P("row", "col")
    return jax.shard_map(body, mesh=mesh, in_specs=in_specs, out_specs=out_specs, check_vma=False)
```

profile of v0, /device:TPU:1, one launch (start us, length us, event | category | flops | bytes accessed | tf_op | source)
XLA Modules:
  0.0 501.4 jit_solution(158808282834339269)
XLA Ops:
  6.5 0.7 all-gather.7.cloned.1.call-update
  7.3 0.7 all-gather.9.cloned.1.call-update
  8.1 0.7 slice.3
  8.8 0.7 select_reduce_fusion
  9.6 0.6 dynamic-slice
  10.2 0.7 dynamic_slice.9
  11.6 0.7 fusion.48
  12.3 51.4 %all-gather.7.cloned.1.call-done = f32[128,8192]{1,0:T(8,128)} async-done(((f32[128,2048]{1,0:T(8,128)}), f32[128,8192]{1,0:T(8,128)}) %all-gather.7.cloned.1.call-update) | async-done | bytes 4194320 | tf_op jit(solution)/shard_map/all_gather | solution.py:52
  63.8 82.7 %all-gather.9.cloned.1.call-done = f32[8192,128]{1,0:T(8,128)} async-done(((f32[128,128]{1,0:T(8,128)}), f32[8192,128]{1,0:T(8,128)}) %all-gather.9.cloned.1.call-update) | async-done | bytes 4194320 | tf_op jit(solution)/shard_map/all_gather | solution.py:59
  146.5 8.4 %fusion.15 = f32[128,128]{1,0:T(8,128)} fusion(f32[8192,128]{1,0:T(8,128)} %all-gather.9.cloned.1.call-done, f32[128,8192]{1,0:T(8,128)} %all-gather.7.cloned.1.call-done, f32[8192]{0:T(1024)S(1)} %broadcast_bitcast_fusion.1, pred[]{:T(512)} %bitcast), kind=kOutput, calls=%fused_computation.16 | convolution fusion | flops 1611677696 | bytes 8486913 | tf_op jit(solution)/shard_map/dot_general | solution.py:57
  155.0 0.6 gather_fusion
  155.6 0.2 fusion.35
  155.8 0.2 fusion.36
  156.0 0.3 fusion.33
  156.3 0.2 fusion.34
  156.7 74.7 %all-gather.11.cloned.1.call-done = f32[8192,128]{1,0:T(8,128)} async-done(((f32[128,128]{1,0:T(8,128)}), f32[8192,128]{1,0:T(8,128)}) %all-gather.11.cloned.1.call-update) | async-done | bytes 4194320 | tf_op jit(solution)/shard_map/all_gather | solution.py:59
  231.4 8.4 %fusion.50 = (f32[128,128]{1,0:T(8,128)}, f32[128,128]{1,0:T(8,128)S(1)}) fusion(f32[128,128]{1,0:T(8,128)S(1)} %copy-done.1, f32[8192,128]{1,0:T(8,128)} %all-gather.11.cloned.1.call-done, f32[128,8192]{1,0:T(8,128)} %all-gather.7.cloned.1.call-done, f32[8192]{0:T(1024)S(1)} %broadcast_bitcast_fusion), kind=kOutput, calls=%fused_computation.55 | convolution fusion | flops 1611677696 | bytes 8617984 | tf_op jit(solution)/shard_map/dot_general | solution.py:57
  239.8 0.2 all-gather.15.cloned.1.call-start
  240.7 75.6 %all-gather.13.cloned.1.call-done = f32[8192,128]{1,0:T(8,128)} async-done(((f32[128,128]{1,0:T(8,128)}), f32[8192,128]{1,0:T(8,128)}) %all-gather.13.cloned.1.call-update) | async-done | bytes 4194320 | tf_op jit(solution)/shard_map/all_gather | solution.py:59
  316.3 8.4 %fusion.18 = f32[128,128]{1,0:T(8,128)} fusion(f32[8192,128]{1,0:T(8,128)} %all-gather.13.cloned.1.call-done, f32[128,8192]{1,0:T(8,128)} %all-gather.7.cloned.1.call-done, f32[8192]{0:T(1024)S(1)} %broadcast_bitcast_fusion.1, pred[]{:T(512)} %bitcast.3), kind=kOutput, calls=%fused_computation.17 | convolution fusion | flops 1611677696 | bytes 8486913 | tf_op jit(solution)/shard_map/dot_general | solution.py:57
  324.8 76.4 %all-gather.15.cloned.1.call-done = f32[8192,128]{1,0:T(8,128)} async-done(((f32[128,128]{1,0:T(8,128)}), f32[8192,128]{1,0:T(8,128)}) %all-gather.15.cloned.1.call-update) | async-done | bytes 4194320 | tf_op jit(solution)/shard_map/all_gather | solution.py:59
  401.2 8.4 %fusion.30 = f32[128,128]{1,0:T(8,128)} fusion(f32[128,128]{1,0:T(8,128)S(1)} %copy-done.1, f32[128,128]{1,0:T(8,128)S(1)} %get-tuple-element.6, f32[8192,128]{1,0:T(8,128)} %all-gather.15.cloned.1.call-done, f32[128,8192]{1,0:T(8,128)} %all-gather.7.cloned.1.call-done, f32[8192]{0:T(1024)S(1)} %broadcast_bitcast_fusion), kind=kOutput, calls=%fused_computation.21 | convolution fusion | flops 1611694080 | bytes 8617984 | tf_op jit(solution)/shard_map/dot_general | solution.py:57
  410.3 75.8 %all-gather.17.cloned.1.call-done = f32[8192,128]{1,0:T(8,128)} async-done(((f32[128,128]{1,0:T(8,128)}), f32[8192,128]{1,0:T(8,128)}) %all-gather.17.cloned.1.call-update) | async-done | bytes 4194320 | tf_op jit(solution)/shard_map/all_gather | solution.py:59
  486.1 8.4 %fusion.24 = f32[128,128]{1,0:T(8,128)} fusion(f32[8192,128]{1,0:T(8,128)} %all-gather.17.cloned.1.call-done, f32[128,8192]{1,0:T(8,128)} %all-gather.7.cloned.1.call-done, f32[8192]{0:T(1024)S(1)} %broadcast_bitcast_fusion.1, f32[128,128]{1,0:T(8,128)S(1)} %copy-done.2, f32[128,128]{1,0:T(8,128)S(1)} %copy-done.3, pred[]{:T(512)} %bitcast.6), kind=kOutput, calls=%fused_computation.19 | convolution fusion | flops 1611710464 | bytes 8617985 | tf_op jit(solution)/shard_map/dot_general | solution.py:57
  (26 shorter events, 0.5 us)
Async XLA Ops:
  6.5 57.2 %all-gather.7.cloned.1.call-start = ((), (), s32[]{:S(2)}) async-start(), calls=%async_computation | async-start | bytes 5242880 | tf_op jit(solution)/shard_map/all_gather | solution.py:52
  7.3 139.2 %all-gather.9.cloned.1.call-start = ((), (), s32[]{:S(2)}) async-start(), calls=%async_computation.1 | async-start | bytes 4259840 | tf_op jit(solution)/shard_map/all_gather | solution.py:59
  8.0 223.4 %all-gather.11.cloned.1.call-start = ((), (), s32[]{:S(2)}) async-start(), calls=%async_computation.2 | async-start | bytes 4259840 | tf_op jit(solution)/shard_map/all_gather | solution.py:59
  146.5 8.5 %copy-start = (s32[7]{0:T(128)S(1)}, s32[7]{0:T(128)}, u32[]{:S(2)}) copy-start(s32[7]{0:T(128)} %param.8) | copy-start | bytes 88
  146.5 9.4 %copy-start.4 = (s32[7,64]{1,0:T(8,128)S(1)}, s32[7,64]{1,0:T(8,128)}, u32[]{:S(2)}) copy-start(s32[7,64]{1,0:T(8,128)} %param.11) | copy-start | bytes 5380
  146.5 84.9 %copy-start.1 = (f32[128,128]{1,0:T(8,128)S(1)}, f32[128,128]{1,0:T(8,128)}, u32[]{:S(2)}) copy-start(f32[128,128]{1,0:T(8,128)} %param.7) | copy-start | bytes 196612
  154.9 161.4 %all-gather.13.cloned.1.call-start = ((), (), s32[]{:S(2)}) async-start(), calls=%async_computation.3 | async-start | bytes 4259840 | tf_op jit(solution)/shard_map/all_gather | solution.py:59
  239.8 161.4 %all-gather.15.cloned.1.call-start = ((), (), s32[]{:S(2)}) async-start(), calls=%async_computation.4 | async-start | bytes 4259840 | tf_op jit(solution)/shard_map/all_gather | solution.py:59
  324.7 161.4 %all-gather.17.cloned.1.call-start = ((), (), s32[]{:S(2)}) async-start(), calls=%async_computation.5 | async-start | bytes 4259840 | tf_op jit(solution)/shard_map/all_gather | solution.py:59
  401.2 84.9 %copy-start.2 = (f32[128,128]{1,0:T(8,128)S(1)}, f32[128,128]{1,0:T(8,128)}, u32[]{:S(2)}) copy-start(f32[128,128]{1,0:T(8,128)} %fusion.15) | copy-start | bytes 196612
  401.2 84.9 %copy-start.3 = (f32[128,128]{1,0:T(8,128)S(1)}, f32[128,128]{1,0:T(8,128)}, u32[]{:S(2)}) copy-start(f32[128,128]{1,0:T(8,128)} %fusion.18) | copy-start | bytes 196612
Sparse Core Ops, SparseCore 0:
  9.2 54.5 all-gather.6
  66.5 79.8 all-gather.8
  155.0 76.3 all-gather.10
  239.9 76.3 all-gather.12
  324.8 76.3 all-gather.14
  409.8 76.3 all-gather.16
where the time goes:
time: 501 us
  waiting for transfers between devices  438 us (87%)
  matrix products  42.9 us (9%)
  between operations  15.6 us (3%)
    all_gather x5, waiting for transfers between devices, product(): lax.all_gather(vector, 'row', axis=0, tiled=True)  385 us
    all_gather x1, waiting for transfers between devices, body(): full_rows = lax.all_gather(factor, 'col', axis=1, tiled=True)  51.4 us
    dot_general x5, matrix products, product(): jnp.dot(matrix, lax.all_gather(vector, 'row', axis=0, tiled=True), precis...  42 us
  transfers between devices with their start and end apart: 6, of which 6 were waited for; matrix products, arithmetic and copies ran while one was open for 1% of the time, Pallas kernels for 0%

commit v1 on v0

--- a/solution.py
+++ b/solution.py
@@ -49,7 +49,12 @@
     level_mine = lax.dynamic_slice_in_dim(level, first, RB, 0)
     same_mine = lax.dynamic_slice_in_dim(same, first, RB, 0)
     link_mine = lax.dynamic_slice_in_dim(link, first, RB, 0)
-    full_rows = lax.all_gather(factor, "col", axis=1, tiled=True)
+    ring = [factor]
+    for hop in range(3):
+        ring.append(lax.ppermute(ring[-1], "col", [(dev, (dev + 1) % 4) for dev in range(4)]))
+    full_rows = jnp.roll(
+        jnp.concatenate(ring[::-1], axis=1), (lax.axis_index("col") + 1) * ring[0].shape[1], axis=1
+    )
     diag_part = masked(full_rows, same_mine)
     link_part = masked(full_rows, link_mine)
 

time: 501 us -> 453 us (0.904)
  waiting for transfers between devices: 438 us -> 375 us
  local copies, waits for them, and re-layouts: 2.79 us -> 13.5 us
  starting transfers between devices: 0.38 us -> 5.41 us
    all_gather x5, waiting for transfers between devices: 385 us -> 313 us  [product(): lax.all_gather(vector, 'row', axis=0, tiled=True)]
    ppermute x0 -> x3, waiting for transfers between devices: none -> 61.4 us  [body(): lax.ppermute(ring[-1], 'col', [(dev, (dev + 1) % 4) for dev in range(4)])]
    all_gather x1 -> x0, waiting for transfers between devices: 51.4 us -> none  [body(): full_rows = lax.all_gather(factor, 'col', axis=1, tiled=True)]
    unnamed x10 -> x19, local copies, waits for them, and re-layouts: 0.02 us -> 9.8 us
  transfers between devices with their start and end apart: 6 -> 8, of which waited for: 6 -> 8; matrix products, arithmetic and copies ran while one was open for 1% -> 4% of each run, Pallas kernels for 0% -> 0%
where the time goes in v1:
time: 453 us
  waiting for transfers between devices  375 us (83%)
  matrix products  42.9 us (9%)
  between operations  15.1 us (3%)
  local copies, waits for them, and re-layouts  13.5 us (3%)
  starting transfers between devices  5.41 us (1%)
    all_gather x5, waiting for transfers between devices, product(): lax.all_gather(vector, 'row', axis=0, tiled=True)  313 us
    ppermute x3, waiting for transfers between devices, body(): lax.ppermute(ring[-1], 'col', [(dev, (dev + 1) % 4) for dev in range(4)])  61.4 us
    dot_general x5, matrix products, product(): jnp.dot(matrix, lax.all_gather(vector, 'row', axis=0, tiled=True), precis...  42 us
    unnamed x19, local copies, waits for them, and re-layouts  9.8 us
  transfers between devices with their start and end apart: 8, of which 8 were waited for; matrix products, arithmetic and copies ran while one was open for 4% of the time, Pallas kernels for 0%

profile of v1, /device:TPU:1, one launch (start us, length us, event | category | flops | bytes accessed | tf_op | source)
XLA Modules:
  0.0 453.2 jit_solution(13086254248390971808)
XLA Ops:
  7.3 2.1 collective-permute-start
  9.4 22.1 %collective-permute-done = f32[128,2048]{1,0:T(8,128)S(1)} collective-permute-done((f32[128,2048]{1,0:T(8,128)}, f32[128,2048]{1,0:T(8,128)S(1)}, u32[]{:S(2)}, u32[]{:S(2)}) %collective-permute-start) | collective-permute-done | bytes 1048608 | tf_op jit(solution)/shard_map/ppermute | solution.py:54
  31.5 1.9 collective-permute-start.1
  33.4 22.0 %collective-permute-done.1 = f32[128,2048]{1,0:T(8,128)S(1)} collective-permute-done((f32[128,2048]{1,0:T(8,128)S(1)}, f32[128,2048]{1,0:T(8,128)S(1)}, u32[]{:S(2)}, u32[]{:S(2)}) %collective-permute-start.1) | collective-permute-done | bytes 1048608 | tf_op jit(solution)/shard_map/ppermute | solution.py:54
  55.4 0.8 collective-permute-start.2
  60.3 17.3 %collective-permute-done.2 = f32[128,2048]{1,0:T(8,128)} collective-permute-done((f32[128,2048]{1,0:T(8,128)S(1)}, f32[128,2048]{1,0:T(8,128)}, u32[]{:S(2)}, u32[]{:S(2)}) %collective-permute-start.2) | collective-permute-done | bytes 1048608 | tf_op jit(solution)/shard_map/ppermute | solution.py:54
  77.6 2.3 constant_dynamic-update-slice_fusion.7
  80.0 1.0 constant_dynamic-update-slice_fusion.6
  81.0 1.1 constant_dynamic-update-slice_fusion.5
  82.1 1.0 constant_dynamic-update-slice_fusion.4
  83.1 2.3 constant_dynamic-update-slice_fusion.3
  85.4 1.0 constant_dynamic-update-slice_fusion.2
  86.4 1.0 constant_dynamic-update-slice_fusion.1
  87.4 1.0 constant_dynamic-update-slice_fusion
  88.5 5.0 %all-gather.6.cloned.1.call-done = f32[8192,128]{1,0:T(8,128)} async-done(((f32[128,128]{1,0:T(8,128)}), f32[8192,128]{1,0:T(8,128)}) %all-gather.6.cloned.1.call-update) | async-done | bytes 4194320 | tf_op jit(solution)/shard_map/all_gather | solution.py:64
  93.5 8.4 %fusion.20 = f32[128,128]{1,0:T(8,128)} fusion(f32[8192,128]{1,0:T(8,128)} %all-gather.6.cloned.1.call-done, f32[128,16384]{1,0:T(8,128)} %constant_dynamic-update-slice_fusion, s32[]{:T(128)S(6)} %select_n.38, f32[8192]{0:T(1024)S(1)} %broadcast_bitcast_fusion.1, pred[]{:T(512)} %bitcast), kind=kOutput, calls=%fused_computation.21 | convolution fusion | flops 1611677696 | bytes 8487428 | tf_op jit(solution)/shard_map/dot_general | solution.py:62
  103.9 79.8 %all-gather.8.cloned.1.call-done = f32[8192,128]{1,0:T(8,128)} async-done(((f32[128,128]{1,0:T(8,128)}), f32[8192,128]{1,0:T(8,128)}) %all-gather.8.cloned.1.call-update) | async-done | bytes 4194320 | tf_op jit(solution)/shard_map/all_gather | solution.py:64
  183.6 8.4 %fusion.60 = (f32[128,128]{1,0:T(8,128)}, f32[128,128]{1,0:T(8,128)S(1)}) fusion(f32[128,128]{1,0:T(8,128)S(1)} %copy-done.2, f32[8192,128]{1,0:T(8,128)} %all-gather.8.cloned.1.call-done, f32[128,16384]{1,0:T(8,128)} %constant_dynamic-update-slice_fusion, s32[]{:T(128)S(6)} %select_n.38, f32[8192]{0:T(1024)S(1)} %broadcast_bitcast_fusion), kind=kOutput, calls=%fused_computation.75 | convolution fusion | flops 1611677696 | bytes 8617988 | tf_op jit(solution)/shard_map/dot_general | solution.py:62
  192.7 75.8 %all-gather.10.cloned.1.call-done = f32[8192,128]{1,0:T(8,128)} async-done(((f32[128,128]{1,0:T(8,128)}), f32[8192,128]{1,0:T(8,128)}) %all-gather.10.cloned.1.call-update) | async-done | bytes 4194320 | tf_op jit(solution)/shard_map/all_gather | solution.py:64
  268.5 8.4 %fusion.23 = f32[128,128]{1,0:T(8,128)} fusion(f32[8192,128]{1,0:T(8,128)} %all-gather.10.cloned.1.call-done, f32[128,16384]{1,0:T(8,128)} %constant_dynamic-update-slice_fusion, s32[]{:T(128)S(6)} %select_n.38, f32[8192]{0:T(1024)S(1)} %broadcast_bitcast_fusion.1, pred[]{:T(512)} %bitcast.3), kind=kOutput, calls=%fused_computation.22 | convolution fusion | flops 1611677696 | bytes 8487428 | tf_op jit(solution)/shard_map/dot_general | solution.py:62
  277.2 76.2 %all-gather.12.cloned.1.call-done = f32[8192,128]{1,0:T(8,128)} async-done(((f32[128,128]{1,0:T(8,128)}), f32[8192,128]{1,0:T(8,128)}) %all-gather.12.cloned.1.call-update) | async-done | bytes 4194320 | tf_op jit(solution)/shard_map/all_gather | solution.py:64
  353.4 8.4 %fusion.32 = f32[128,128]{1,0:T(8,128)} fusion(f32[128,128]{1,0:T(8,128)S(1)} %copy-done.2, f32[128,128]{1,0:T(8,128)S(1)} %get-tuple-element.6, f32[8192,128]{1,0:T(8,128)} %all-gather.12.cloned.1.call-done, f32[128,16384]{1,0:T(8,128)} %constant_dynamic-update-slice_fusion, s32[]{:T(128)S(6)} %select_n.38, f32[8192]{0:T(1024)S(1)} %broadcast_bitcast_fusion), kind=kOutput, calls=%fused_computation.25 | convolution fusion | flops 1611694080 | bytes 8617988 | tf_op jit(solution)/shard_map/dot_general | solution.py:62
  362.5 75.8 %all-gather.14.cloned.1.call-done = f32[8192,128]{1,0:T(8,128)} async-done(((f32[128,128]{1,0:T(8,128)}), f32[8192,128]{1,0:T(8,128)}) %all-gather.14.cloned.1.call-update) | async-done | bytes 4194320 | tf_op jit(solution)/shard_map/all_gather | solution.py:64
  438.3 8.4 %add_add_fusion = f32[128,128]{1,0:T(8,128)} fusion(f32[128,128]{1,0:T(8,128)S(1)} %copy-done.3, f32[128,128]{1,0:T(8,128)S(1)} %copy-done.4, f32[8192,128]{1,0:T(8,128)} %all-gather.14.cloned.1.call-done, f32[128,16384]{1,0:T(8,128)} %constant_dynamic-update-slice_fusion, s32[]{:T(128)S(6)} %select_n.38, f32[8192]{0:T(1024)S(1)} %broadcast_bitcast_fusion.1, ...), kind=kOutput, calls=%fused_computation.26 | convolution fusion | flops 1611710464 | bytes 8618500 | tf_op jit(solution)/shard_map/dot_general | solution.py:62
  (39 shorter events, 6.5 us)
Async XLA Ops:
  6.5 75.5 %copy-start.1 = (f32[128,2048]{1,0:T(8,128)S(1)}, f32[128,2048]{1,0:T(8,128)}, u32[]{:S(2)}) copy-start(f32[128,2048]{1,0:T(8,128)} %param.6) | copy-start | bytes 3145732
  6.5 87.0 %all-gather.6.cloned.1.call-start = ((), (), s32[]{:S(2)}) async-start(), calls=%async_computation | async-start | bytes 4259840 | tf_op jit(solution)/shard_map/all_gather | solution.py:64
  7.3 176.4 %all-gather.8.cloned.1.call-start = ((), (), s32[]{:S(2)}) async-start(), calls=%async_computation.1 | async-start | bytes 4259840 | tf_op jit(solution)/shard_map/all_gather | solution.py:64
  7.3 24.2 %collective-permute-start = (f32[128,2048]{1,0:T(8,128)}, f32[128,2048]{1,0:T(8,128)S(1)}, u32[]{:S(2)}, u32[]{:S(2)}) collective-permute-start(f32[128,2048]{1,0:T(8,128)} %param.6), channel_id=1, source_target_pairs={{0,1},{1,2},{2,3},{3,0},{4,5},{5,6},{6,7},{7,4},{8,9},{9,10},{10,1... | collective-permute-start | bytes 3145736 | tf_op jit(solution)/shard_map/ppermute | solution.py:54
  31.5 23.9 %collective-permute-start.1 = (f32[128,2048]{1,0:T(8,128)S(1)}, f32[128,2048]{1,0:T(8,128)S(1)}, u32[]{:S(2)}, u32[]{:S(2)}) collective-permute-start(f32[128,2048]{1,0:T(8,128)S(1)} %collective-permute-done), channel_id=1, source_target_pairs={{0,1},{1,2},{2,3},{3,0},{4,5},{5,6},{6,7},{7,4},{8,9},{9,10},{10,1... | collective-permute-start | bytes 3145736 | tf_op jit(solution)/shard_map/ppermute | solution.py:54
  55.4 22.3 %collective-permute-start.2 = (f32[128,2048]{1,0:T(8,128)S(1)}, f32[128,2048]{1,0:T(8,128)}, u32[]{:S(2)}, u32[]{:S(2)}) collective-permute-start(f32[128,2048]{1,0:T(8,128)S(1)} %collective-permute-done.1), channel_id=1, source_target_pairs={{0,1},{1,2},{2,3},{3,0},{4,5},{5,6},{6,7},{7,4},{8,9},{9,10},{10,1... | collective-permute-start | bytes 3145736 | tf_op jit(solution)/shard_map/ppermute | solution.py:54
  93.5 8.7 %copy-start = (s32[7]{0:T(128)S(1)}, s32[7]{0:T(128)}, u32[]{:S(2)}) copy-start(s32[7]{0:T(128)} %param.8) | copy-start | bytes 88
  93.5 9.6 %copy-start.5 = (s32[7,64]{1,0:T(8,128)S(1)}, s32[7,64]{1,0:T(8,128)}, u32[]{:S(2)}) copy-start(s32[7,64]{1,0:T(8,128)} %param.11) | copy-start | bytes 5380
  93.5 90.1 %copy-start.2 = (f32[128,128]{1,0:T(8,128)S(1)}, f32[128,128]{1,0:T(8,128)}, u32[]{:S(2)}) copy-start(f32[128,128]{1,0:T(8,128)} %param.7) | copy-start | bytes 196612
  101.9 166.6 %all-gather.10.cloned.1.call-start = ((), (), s32[]{:S(2)}) async-start(), calls=%async_computation.2 | async-start | bytes 4259840 | tf_op jit(solution)/shard_map/all_gather | solution.py:64
  192.0 161.4 %all-gather.12.cloned.1.call-start = ((), (), s32[]{:S(2)}) async-start(), calls=%async_computation.3 | async-start | bytes 4259840 | tf_op jit(solution)/shard_map/all_gather | solution.py:64
  276.9 161.4 %all-gather.14.cloned.1.call-start = ((), (), s32[]{:S(2)}) async-start(), calls=%async_computation.4 | async-start | bytes 4259840 | tf_op jit(solution)/shard_map/all_gather | solution.py:64
  353.4 84.9 %copy-start.3 = (f32[128,128]{1,0:T(8,128)S(1)}, f32[128,128]{1,0:T(8,128)}, u32[]{:S(2)}) copy-start(f32[128,128]{1,0:T(8,128)} %fusion.20) | copy-start | bytes 196612
  353.4 84.9 %copy-start.4 = (f32[128,128]{1,0:T(8,128)S(1)}, f32[128,128]{1,0:T(8,128)}, u32[]{:S(2)}) copy-start(f32[128,128]{1,0:T(8,128)} %fusion.23) | copy-start | bytes 196612
Sparse Core Ops, SparseCore 0:
  10.1 83.3 all-gather.5
  102.1 81.5 all-gather.7
  192.2 76.3 all-gather.9
  277.0 76.3 all-gather.11
  362.0 76.3 all-gather.13
